TPU v7x, 1024 devices: a whole 4x8x16 slice. The times are simulated.
1024 devices in a mesh: ctx: 16 (over z_lo, core), tp: 64 (over y, z_hi, x).
Axes of the slice: x: 4, y: 8, z: 16 (z_hi: 2, z_lo: 8; z = z_hi * 8 + z_lo), core: 2. Of those that a mesh axis runs over, the one named last changes fastest.
Arguments:
- lin_query: bfloat16 [8192, 64, 128], P('ctx', 'tp'), may hold values from -6 to 6
- lin_key: bfloat16 [8192, 64, 128], P('ctx', 'tp'), may hold values from -6 to 6
- lin_value: bfloat16 [8192, 64, 128], P('ctx', 'tp'), may hold values from -6 to 6
- log_decay: float32 [64, 8192], P('tp', 'ctx'), may hold values from -2 to 0, as said below
- soft_query: bfloat16 [8192, 64, 128], P('ctx', 'tp'), may hold values from -12 to 12
- soft_key: bfloat16 [8192, 64, 128], P('ctx', 'tp'), may hold values from -4 to 4
- soft_value: bfloat16 [8192, 64, 128], P('ctx', 'tp'), may hold values from -6 to 6
Outputs:
- linear_out: bfloat16 [8192, 64, 128], P('ctx', 'tp')
- softmax_out: bfloat16 [8192, 64, 128], P('ctx', 'tp')
Inputs may be any that keep to these rules, and one draw needn't show every extreme that they name: `log_decay`: every entry is negative.
All inputs are finite; a program needn't handle non-finite values.
Results may differ from a plain program's by a relative error of at most 0.0055.
Values may be sent and summed in bfloat16 or wider, within the bound.
A program may use at most 32 MiB of HBM per device.

v0:
```python
import math

import jax
import jax.numpy as jnp
from jax import lax
from jax.sharding import PartitionSpec as P


def entering(shard, axis, combine, identity):
    peers, position = (lax.axis_size(axis), lax.axis_index(axis))
    everything = jax.tree.map(lambda part: lax.all_gather(part, axis), shard)
    start = jax.tree.map(
        lambda part, zero: jnp.broadcast_to(jnp.asarray(zero, part.dtype), part.shape),
        shard,
        identity,
    )

    def hop(k, before):
        reached = k < position
        new = combine(before, jax.tree.map(lambda part: part[k], everything))
        return jax.tree.map(lambda a, b: jnp.where(reached, a, b), new, before)

    return lax.fori_loop(0, peers, hop, start)


def combine_states(earlier, later):
    return (earlier[0] * later[0], later[0][:, None, None] * earlier[1] + later[1])


def lightning_block(lin_query, lin_key, lin_value, log_decay):
    rows = lin_query.shape[0]
    heads = lin_query.shape[1]
    width = lin_query.shape[2]
    cum = jnp.cumsum(log_decay, axis=1)
    lower = jnp.arange(rows)[:, None] >= jnp.arange(rows)[None, :]
    diff = cum[:, :, None] - cum[:, None, :]
    mask = jnp.exp(jnp.where(lower[None], diff, -1e30))
    scores = jnp.einsum("thd,shd->hts", lin_query, lin_key, preferred_element_type=jnp.float32)
    weights = (scores * mask).astype(jnp.bfloat16)
    intra = jnp.einsum("hts,she->the", weights, lin_value, preferred_element_type=jnp.float32)
    last = cum[:, -1]
    decayed = (lin_key.astype(jnp.float32) * jnp.exp(last[None, :] - cum.T)[:, :, None]).astype(
        jnp.bfloat16
    )
    local_state = jnp.einsum("thd,the->hde", decayed, lin_value, preferred_element_type=jnp.float32)
    empty = jnp.zeros((heads, width, width), jnp.float32)
    identity = (jnp.ones((heads,), jnp.float32), empty)
    factor, carried = entering((jnp.exp(last), local_state), "ctx", combine_states, identity)
    inter = jnp.einsum(
        "thd,hde->the", lin_query, carried.astype(jnp.bfloat16), preferred_element_type=jnp.float32
    )
    raw = intra + inter * jnp.exp(cum).T[:, :, None]
    normed = raw * lax.rsqrt(jnp.mean(raw * raw, axis=-1, keepdims=True) + 1e-06)
    return normed.astype(jnp.bfloat16)


def tile_update(query, query_pos, keys, values, key_start, scale, state):
    running, total, summed = state
    block = keys.shape[0]
    scores = jnp.einsum("thd,shd->hts", query, keys, preferred_element_type=jnp.float32) * scale
    allowed = (query_pos[:, None] >= key_start + jnp.arange(block)[None, :])[None]
    scores = jnp.where(allowed, scores, -1e30)
    updated = jnp.maximum(running, jnp.max(scores, axis=-1))
    probs = jnp.where(allowed, jnp.exp(scores - updated[:, :, None]), 0.0)
    correction = jnp.exp(running - updated)
    total = total * correction + jnp.sum(probs, axis=-1)
    decay_product = jnp.einsum(
        "hts,she->the", probs.astype(jnp.bfloat16), values, preferred_element_type=jnp.float32
    )
    summed = summed * correction.T[:, :, None] + decay_product
    return (updated, total, summed)


def fresh_state(heads, count, width):
    return (
        jnp.full((heads, count), -1e30, jnp.float32),
        jnp.zeros((heads, count), jnp.float32),
        jnp.zeros((count, heads, width), jnp.float32),
    )


def softmax_block(soft_query, soft_key, soft_value):
    rows = soft_query.shape[0]
    heads = soft_query.shape[1]
    width = soft_query.shape[2]
    scale = 1.0 / math.sqrt(width)
    position = lax.axis_index("ctx")
    first_row = position * rows
    query_pos = first_row + jnp.arange(rows)
    start_state = fresh_state(heads, rows, width)
    key_piece = lax.all_gather(soft_key, "ctx", axis=0, tiled=True)
    value_piece = lax.all_gather(soft_value, "ctx", axis=0, tiled=True)
    length = key_piece.shape[0]
    block = math.gcd(512, length)

    def one_tile(step, state):
        keys = lax.dynamic_slice_in_dim(key_piece, step * block, block, 0)
        values = lax.dynamic_slice_in_dim(value_piece, step * block, block, 0)
        key_start = step * block
        return tile_update(soft_query, query_pos, keys, values, key_start, scale, state)

    combined_summary = lax.fori_loop(0, length // block, one_tile, start_state)
    running, total, summed = combined_summary
    return (summed / total.T[:, :, None]).astype(jnp.bfloat16)


def on_device(lin_query, lin_key, lin_value, log_decay, soft_query, soft_key, soft_value):
    linear_out = lightning_block(lin_query, lin_key, lin_value, log_decay)
    softmax_out = softmax_block(soft_query, soft_key, soft_value)
    return (linear_out, softmax_out)


def solution(mesh):
    return jax.shard_map(
        on_device,
        mesh=mesh,
        in_specs=(
            P("ctx", "tp", None),
            P("ctx", "tp", None),
            P("ctx", "tp", None),
            P("tp", "ctx"),
            P("ctx", "tp", None),
            P("ctx", "tp", None),
            P("ctx", "tp", None),
        ),
        out_specs=(P("ctx", "tp", None), P("ctx", "tp", None)),
        check_vma=False,
    )
```

profile of v0, /device:TPU:1, one launch (start us, length us, event | category | flops | bytes accessed | tf_op | source)
XLA Modules:
  0.0 392.0 jit_solution(943294770655540103)
XLA Ops:
  7.2 1.0 reduce-window.6
  11.2 1.9 fusion.36
  13.2 0.7 all-gather.5.cloned.1.call-update
  14.0 0.7 all-gather.7.cloned.1.call-update
  14.8 1.3 dynamic-slice
  16.1 0.7 bitcast_dynamic-update-slice_fusion
  16.7 58.9 %all-reduce = f32[16]{0:T(128)S(1)} all-reduce(f32[16]{0:T(128)S(1)} %bitcast_dynamic-update-slice_fusion), channel_id=1, replica_groups=mesh['ctx'=16,'tp'=64] {'ctx'}, use_global_device_ids=true, to_apply=%add | all-reduce | flops 16 | bytes 128
  75.7 1.5 fusion.26
  77.2 46.8 %all-gather.9.cloned.1.call-done = f32[2048,128]{1,0:T(8,128)} async-done(((f32[128,128]{1,0:T(8,128)}), f32[2048,128]{1,0:T(8,128)}) %all-gather.9.cloned.1.call-update) | async-done | bytes 1048592 | tf_op jit(solution)/shard_map/all_gather | solution.py:11
  124.0 33.8 %while.32 = (s32[]{:T(128)}, f32[1,128,128]{2,1,0:T(8,128)S(1)}, s32[]{:T(128)}, f32[16,1]{0,1:T(1,128)S(1)}, f32[16,1,128,128]{3,2,1,0:T(8,128)}, /*index=5*/s32[]{:T(128)}, s32[]{:T(128)}) while((s32[]{:T(128)}, f32[1,128,128]{2,1,0:T(8,128)S(1)}, s32[]{:T(128)}, f32[16,1]{0,1:T(1,128)S(1)}, f32[16,1,128,128]{3,2,1,0:T(8,128)}, ...), condition=%wide.region_3.4_spmd.clone, body=%wide.region_2.3_spmd.clone.sunk | while | flops 65540 | bytes 196733 | solution.py:23
  124.6 1.5 fusion.59
  126.7 1.5 fusion.59
  128.2 0.6 constant_dynamic-slice_fusion.2
  128.8 1.5 fusion.59
  130.9 1.5 fusion.59
  133.1 1.5 fusion.59
  135.2 1.5 fusion.59
  137.3 1.5 fusion.59
  139.4 1.5 fusion.59
  141.5 1.5 fusion.59
  143.6 1.5 fusion.59
  145.7 1.5 fusion.59
  147.8 1.5 fusion.59
  149.9 1.5 fusion.59
  152.1 1.5 fusion.59
  154.2 1.5 fusion.59
  156.3 1.5 fusion.59
  158.1 0.8 copy.16
  158.8 72.2 %all-gather.5.cloned.1.call-done = bf16[8192,1,128]{2,0,1:T(8,128)(2,1)} async-done(((bf16[512,1,128]{2,0,1:T(8,128)(2,1)}), bf16[8192,1,128]{2,0,1:T(8,128)(2,1)}) %all-gather.5.cloned.1.call-update) | async-done | bytes 2097168 | tf_op jit(solution)/shard_map/all_gather | solution.py:91
  231.1 107.3 %all-gather.7.cloned.1.call-done = bf16[8192,1,128]{2,0,1:T(8,128)(2,1)} async-done(((bf16[512,1,128]{2,0,1:T(8,128)(2,1)}), bf16[8192,1,128]{2,0,1:T(8,128)(2,1)}) %all-gather.7.cloned.1.call-update) | async-done | bytes 2097168 | tf_op jit(solution)/shard_map/all_gather | solution.py:92
  338.3 46.2 %while.33 = (s32[]{:T(128)}, f32[1,512]{1,0:T(1,128)S(1)}, f32[1,512]{1,0:T(1,128)S(1)}, f32[512,1,128]{0,2,1:T(8,128)S(1)}, bf16[8192,1,128]{2,0,1:T(8,128)(2,1...) while((s32[]{:T(128)}, f32[1,512]{1,0:T(1,128)S(1)}, ...), condition=%wide.region_8.9_spmd.clone, body=%wide.region_5.8_spmd.clone.sunk | while | flops 137563648 | bytes 4112583 | solution.py:102
  338.3 1.2 fusion.62
  339.8 1.3 fusion.66
  341.2 1.2 fusion.62
  342.7 1.3 fusion.66
  344.1 1.2 fusion.62
  345.6 1.3 fusion.66
  347.0 1.2 fusion.62
  348.5 1.3 fusion.66
  349.9 1.2 fusion.62
  351.4 1.3 fusion.66
  352.8 1.2 fusion.62
  354.3 1.3 fusion.66
  355.6 1.2 fusion.62
  357.2 1.3 fusion.66
  358.5 1.2 fusion.62
  360.0 1.3 fusion.66
  361.4 1.2 fusion.62
  362.9 1.3 fusion.66
  364.3 1.2 fusion.62
  365.8 1.3 fusion.66
  367.2 1.2 fusion.62
  368.7 1.3 fusion.66
  370.1 1.2 fusion.62
  371.6 1.3 fusion.66
  373.0 1.2 fusion.62
  374.5 1.3 fusion.66
  375.9 1.2 fusion.62
  377.4 1.3 fusion.66
  378.8 1.2 fusion.62
  380.3 1.3 fusion.66
  381.6 1.2 fusion.62
  383.2 1.3 fusion.66
  384.6 0.8 divide_convert_fusion
  (120 shorter events, 15.4 us)
Async XLA Ops:
  7.2 68.5 %copy-start = (bf16[512,1,128]{2,0,1:T(8,128)(2,1)S(1)}, bf16[512,1,128]{2,0,1:T(8,128)(2,1)}, u32[]{:S(2)}) copy-start(bf16[512,1,128]{2,0,1:T(8,128)(2,1)} %param.11) | copy-start | bytes 393220
  7.2 116.8 %all-gather.9.cloned.1.call-start = ((), (), s32[]{:S(2)}) async-start(), calls=%async_computation.2 | async-start | bytes 1114112 | tf_op jit(solution)/shard_map/all_gather | solution.py:11
  13.2 217.9 %all-gather.5.cloned.1.call-start = ((), (), s32[]{:S(2)}) async-start(), calls=%async_computation | async-start | bytes 2228224 | tf_op jit(solution)/shard_map/all_gather | solution.py:91
  13.9 324.4 %all-gather.7.cloned.1.call-start = ((), (), s32[]{:S(2)}) async-start(), calls=%async_computation.1 | async-start | bytes 2228224 | tf_op jit(solution)/shard_map/all_gather | solution.py:92
  75.7 262.7 %copy-start.1 = (bf16[512,1,128]{2,0,1:T(8,128)(2,1)S(1)}, bf16[512,1,128]{2,0,1:T(8,128)(2,1)}, u32[]{:S(2)}) copy-start(bf16[512,1,128]{2,0,1:T(8,128)(2,1)} %param.15) | copy-start | bytes 393220
Sparse Core Ops, SparseCore 0:
  13.3 110.6 all-gather.8
  126.7 104.3 all-gather.4
  233.7 104.5 all-gather.6
where the time goes:
time: 394 us; the launch traced here: 392 us
  waiting for transfers between devices  228 us (58%)
  blocking collectives  58.9 us (15%)
  matrix products  44.5 us (11%)
  other arithmetic  30.5 us (8%)
  between operations  15.2 us (4%)
  local copies, waits for them, and re-layouts  13.7 us (3%)
    all_gather x1, waiting for transfers between devices, softmax_block(): value_piece = lax.all_gather(soft_value, 'ctx', axis=0, tiled=True)  107 us
    all_gather x1, waiting for transfers between devices, softmax_block(): key_piece = lax.all_gather(soft_key, 'ctx', axis=0, tiled=True)  72.2 us
    unnamed x1, blocking collectives  58.9 us
    all_gather x1, waiting for transfers between devices, entering(): everything = jax.tree.map(lambda part: lax.all_gather(part, axis), shard)  46.8 us
    select_n x16, other arithmetic, hop(): return jax.tree.map(lambda a, b: jnp.where(reached, a, b), new, before)  24.1 us
    dot_general x16, matrix products, tile_update(): jnp.einsum('hts,she->the', probs.astype(jnp.bfloat16), values, preferred_...  21.1 us
    dot_general x16, matrix products, tile_update(): jnp.einsum('thd,shd->hts', query, keys, preferred_element_type=jnp.float32)  19.7 us
    dynamic_slice x16, local copies, waits for them, and re-layouts, hop(): new = combine(before, jax.tree.map(lambda part: part[k], everything))  9.35 us
  transfers between devices with their start and end apart: 3, of which 3 were waited for; matrix products, arithmetic and copies ran while one was open for 10% of the time, Pallas kernels for 0%

commit v1 on v0

v1 whole, which is shorter than its diff:
```python
import functools
import math

import jax
import jax.numpy as jnp
from jax import lax
from jax.experimental import pallas as pl
from jax.experimental.pallas import tpu as pltpu
from jax.sharding import PartitionSpec as P

MESH = pl.DeviceIdType.MESH
ROWS = 512
E = 128
CHIPS = 8
TILE = 128
RELAY = 2
SCALE = 1.0 / math.sqrt(E)
NEG = -1e30
WRAP = True


def dot_nt(a, b):
    return lax.dot_general(a, b, (((1,), (1,)), ((), ())), preferred_element_type=jnp.float32)


def dot_tn(a, b):
    return lax.dot_general(a, b, (((0,), (0,)), ((), ())), preferred_element_type=jnp.float32)


def dot_nn(a, b):
    return jnp.dot(a, b, preferred_element_type=jnp.float32)


def kernel(
    lq, lk, lv, ld, sq, sk, sv,
    lin_out, soft_out,
    kv, relay, top, total, summed, intra, cumcol, state, sib_state, carry, onward,
    own_sem, up_send, z_recv, sib_send, sib_recv, ring_send, ring_recv, x_send, x_recv,
    c_send, c_recv,
):
    me = lax.axis_index("ctx")
    tp = lax.axis_index("tp")
    k = me // 2
    c = me % 2
    sib = me + 1 - 2 * c
    other = tp + 4 - 8 * ((tp // 4) % 2)

    def first_up(chip):
        return jnp.maximum(chip - 5, 0) if WRAP else 0 * chip

    def to(ctx, group=None):
        return {"ctx": ctx} if group is None else {"ctx": ctx, "tp": group}

    barrier = pltpu.get_barrier_semaphore()

    def greet(device):
        pl.semaphore_signal(barrier, inc=1, device_id=device, device_id_type=MESH)

    greet(to(sib))

    @pl.when(k < CHIPS - 1)
    def _():
        greet(to(me + 2))

    @pl.when(k > 0)
    def _():
        greet(to(me - 2))

    expected = 1 + jnp.where(k < CHIPS - 1, 1, 0) + jnp.where(k > 0, 1, 0)
    if WRAP:
        @pl.when(k < 2)
        def _():
            greet(to(2 * RELAY + c, other))

        @pl.when(k == CHIPS - 1)
        def _():
            greet(to(2 * RELAY + c, other))

        @pl.when(k == RELAY)
        def _():
            greet(to(c, other))
            greet(to(2 + c, other))
            greet(to(2 * CHIPS - 2 + c, other))

        expected = expected + jnp.where(k < 2, 1, 0) + jnp.where(k == CHIPS - 1, 1, 0)
        expected = expected + jnp.where(k == RELAY, 3, 0)
    pl.semaphore_wait(barrier, expected)

    def remote(src, dst, send, recv, device):
        return pltpu.make_async_remote_copy(
            src_ref=src, dst_ref=dst, send_sem=send, recv_sem=recv,
            device_id=device, device_id_type=MESH,
        )

    def up_copy(src, b, t):
        return remote(src, kv.at[2 * b + c, t], up_send.at[b, t], z_recv.at[b, t], to(me + 2))

    def down_copy(src, b, t):
        return remote(src, kv.at[2 * b + c, t], up_send.at[b, t], z_recv.at[b, t], to(me - 2))

    def sib_copy(src, b, t):
        return remote(src, kv.at[2 * b + c, t], sib_send.at[b, t], sib_recv.at[b, t], to(sib))

    def ring_copy(src, t):
        return remote(
            src, relay.at[k, t], ring_send.at[0, t], ring_recv.at[k, t],
            to(2 * RELAY + c, other),
        )

    def relay_copy(b, t):
        return remote(
            relay.at[b, t], kv.at[2 * b + c, t], ring_send.at[b, t], z_recv.at[b, t],
            to(2 * CHIPS - 2 + c, other),
        )

    own = (sk, sv)
    for t in range(2):
        @pl.when(k < CHIPS - 1)
        def _(t=t):
            up_copy(own[t], k, t).start()

        if WRAP:
            @pl.when(k < 2)
            def _(t=t):
                ring_copy(own[t], t).start()

        @pl.when(c == 0)
        def _(t=t):
            sib_copy(own[t], k, t).start()

    for t in range(2):
        pltpu.make_async_copy(own[t], kv.at[me, t], own_sem.at[t]).start()

    cum = jnp.broadcast_to(ld[...], (8, ROWS))
    lane = lax.broadcasted_iota(jnp.int32, (8, ROWS), 1)
    shift = 1
    while shift < ROWS:
        cum = cum + jnp.where(lane >= shift, pltpu.roll(cum, shift, 1), 0.0)
        shift *= 2
    row = cum[0:1]
    cumcol[...] = jnp.transpose(jnp.broadcast_to(row, (E, ROWS)))
    last = cumcol[ROWS - 1:ROWS, :]
    decayed = (lk[...].astype(jnp.float32) * jnp.exp(last - cumcol[...])).astype(jnp.bfloat16)
    state[0:E, :] = dot_tn(decayed, lv[...])
    state[E:E + 8, :] = jnp.broadcast_to(jnp.exp(last), (8, E))
    exchange = remote(state, sib_state, x_send, x_recv, to(sib))
    exchange.start()

    lower = (
        lax.broadcasted_iota(jnp.int32, (TILE, TILE), 0)
        >= lax.broadcasted_iota(jnp.int32, (TILE, TILE), 1)
    )
    for r in range(ROWS // TILE):
        mine = slice(r * TILE, (r + 1) * TILE)
        part = jnp.zeros((TILE, E), jnp.float32)
        for s in range(r + 1):
            theirs = slice(s * TILE, (s + 1) * TILE)
            diff = cumcol[mine, :] - row[:, theirs]
            if s == r:
                diff = jnp.where(lower, diff, NEG)
            weight = (dot_nt(lq[mine, :], lk[theirs, :]) * jnp.exp(diff)).astype(jnp.bfloat16)
            part = part + dot_nn(weight, lv[theirs, :])
        intra[mine, :] = part

    for t in range(2):
        pltpu.make_async_copy(own[t], kv.at[me, t], own_sem.at[t]).wait()
    for r in range(ROWS // TILE):
        mine = slice(r * TILE, (r + 1) * TILE)
        reach = (r + 1) * TILE
        score = dot_nt(sq[mine, :], kv[me, 0, 0:reach, :]) * SCALE
        allowed = (
            lax.broadcasted_iota(jnp.int32, (TILE, reach), 0) + r * TILE
            >= lax.broadcasted_iota(jnp.int32, (TILE, reach), 1)
        )
        score = jnp.where(allowed, score, NEG)
        peak = jnp.broadcast_to(jnp.max(score, axis=1, keepdims=True), (TILE, E))
        prob = jnp.exp(score - jnp.concatenate([peak] * (r + 1), axis=1))
        top[mine, :] = peak
        total[mine, :] = jnp.broadcast_to(jnp.sum(prob, axis=1, keepdims=True), (TILE, E))
        summed[mine, :] = dot_nn(prob.astype(jnp.bfloat16), kv[me, 1, 0:reach, :])

    def update(slot):
        keys = kv[slot, 0]
        values = kv[slot, 1]
        for r in range(ROWS // TILE):
            mine = slice(r * TILE, (r + 1) * TILE)
            score = dot_nt(sq[mine, :], keys) * SCALE
            before = top[mine, :]
            peak = jnp.maximum(before, jnp.max(score, axis=1, keepdims=True))
            prob = jnp.exp(score - jnp.concatenate([peak] * (ROWS // E), axis=1))
            fade = jnp.exp(before - peak)
            top[mine, :] = peak
            total[mine, :] = total[mine, :] * fade + jnp.sum(prob, axis=1, keepdims=True)
            summed[mine, :] = summed[mine, :] * fade + dot_nn(prob.astype(jnp.bfloat16), values)

    @pl.when(c == 1)
    def _():
        for t in range(2):
            sib_copy(kv.at[me - 1, t], k, t).wait_recv()
        update(me - 1)

    exchange.wait_recv()
    half = E // 2

    def up_carry():
        return remote(
            onward, carry.at[pl.ds(c * half, half)], c_send.at[0], c_recv.at[0], to(me + 2)
        )

    def side_carry():
        return remote(
            carry.at[pl.ds(c * half, half)], carry.at[pl.ds(c * half, half)],
            c_send.at[1], c_recv.at[1], to(sib),
        )

    def chip_state():
        even = jnp.where(c == 0, 1.0, 0.0)
        odd = 1.0 - even
        f_me = state[E:E + 1, :]
        f_sib = sib_state[E:E + 1, :]
        mine = state[pl.ds(c * half, half), :]
        theirs = sib_state[pl.ds(c * half, half), :]
        f_odd = f_me * odd + f_sib * even
        s_even = mine * even + theirs * odd
        s_odd = mine * odd + theirs * even
        return f_me * f_sib, f_odd * s_even + s_odd

    @pl.when(k == 0)
    def _():
        carry[...] = jnp.zeros((E, E), jnp.float32)
        onward[...] = chip_state()[1]
        up_carry().start()

    def pass_carry():
        up_carry().wait_recv()
        side_carry().start()

        @pl.when(k < CHIPS - 1)
        def _():
            factor, added = chip_state()
            onward[...] = factor * carry[pl.ds(c * half, half), :] + added
            up_carry().start()

    carry_step = (k + 2) // 2 + 3 * (k // 7)

    def sends_up(b):
        return (k < CHIPS - 1) & (b >= first_up(k + 1))

    def step(s, _):
        b = k - s
        if WRAP:
            b7 = jnp.where(s <= 3, 7 - s, jnp.where(s <= 5, s - 4, 9 - s))
            b6 = jnp.where(s <= 4, 6 - s, s - 5)
            b = jnp.where(k == 7, b7, jnp.where(k == 6, b6, b))
        for t in range(2):
            up_copy(kv.at[2 * b + c, t], b, t).wait_recv()

            @pl.when(sends_up(b))
            def _(t=t):
                up_copy(kv.at[2 * b + c, t], b, t).start()

            if WRAP:
                @pl.when((k == CHIPS - 1) & (b == 0))
                def _(t=t):
                    down_copy(kv.at[2 * b + c, t], b, t).start()

            sib_copy(kv.at[2 * b + c, t], b, t).start()
        update(2 * b + c)
        for t in range(2):
            sib_copy(kv.at[2 * b + 1 - c, t], b, t).wait_recv()
        update(2 * b + 1 - c)

        @pl.when(s == carry_step)
        def _():
            pass_carry()

        return 0

    lax.fori_loop(1, k + 1, step, 0)

    if WRAP:
        @pl.when(k == RELAY)
        def _():
            for b in range(2):
                for t in range(2):
                    ring_arrival = remote(
                        own[t], relay.at[b, t], ring_send.at[b, t], ring_recv.at[b, t], to(sib)
                    )
                    ring_arrival.wait_recv()
                    relay_copy(b, t).start()

    for r in range(ROWS // TILE):
        mine = slice(r * TILE, (r + 1) * TILE)
        soft_out[mine, :] = (summed[mine, :] / total[mine, :]).astype(soft_out.dtype)

    @pl.when(k > 0)
    def _():
        side_carry().wait_recv()

    even = jnp.where(c == 0, 1.0, 0.0)
    odd = 1.0 - even
    f_sib = sib_state[E:E + 1, :]
    entering = (
        carry[...] * (even + odd * f_sib) + odd * sib_state[0:E, :]
    ).astype(jnp.bfloat16)
    for r in range(ROWS // TILE):
        mine = slice(r * TILE, (r + 1) * TILE)
        raw = intra[mine, :] + dot_nn(lq[mine, :], entering) * jnp.exp(cumcol[mine, :])
        mean = jnp.mean(raw * raw, axis=1, keepdims=True)
        lin_out[mine, :] = (raw * lax.rsqrt(mean + 1e-06)).astype(lin_out.dtype)

    exchange.wait_send()

    @pl.when(k < CHIPS - 1)
    def _():
        up_carry().wait_send()

    @pl.when(k > 0)
    def _():
        side_carry().wait_send()

    def drain(b, _):
        for t in range(2):
            @pl.when(sends_up(b))
            def _(t=t):
                up_copy(kv.at[2 * b + c, t], b, t).wait_send()

            if WRAP:
                @pl.when((k == CHIPS - 1) & (b == 0))
                def _(t=t):
                    down_copy(kv.at[2 * b + c, t], b, t).wait_send()

            @pl.when((b < k) | (c == 0))
            def _(t=t):
                sib_copy(kv.at[2 * b + c, t], b, t).wait_send()
        return 0

    lax.fori_loop(0, k + 1, drain, 0)
    if WRAP:
        @pl.when(k < 2)
        def _():
            for t in range(2):
                ring_copy(own[t], t).wait_send()

        @pl.when(k == RELAY)
        def _():
            for b in range(2):
                for t in range(2):
                    relay_copy(b, t).wait_send()


def on_device(lin_query, lin_key, lin_value, log_decay, soft_query, soft_key, soft_value):
    def flat(array):
        return array.reshape(ROWS, E)

    vmem = pl.BlockSpec(memory_space=pltpu.VMEM)
    hbm = pl.BlockSpec(memory_space=pl.ANY)
    f32, bf16 = jnp.float32, jnp.bfloat16
    dma = pltpu.SemaphoreType.DMA
    lin, soft = pl.pallas_call(
        kernel,
        out_shape=[jax.ShapeDtypeStruct((ROWS, E), bf16)] * 2,
        in_specs=[vmem] * 5 + [hbm] * 2,
        out_specs=[vmem] * 2,
        scratch_shapes=[
            pltpu.VMEM((2 * CHIPS, 2, ROWS, E), bf16),
            pltpu.VMEM((2, 2, ROWS, E), bf16),
            pltpu.VMEM((ROWS, E), f32),
            pltpu.VMEM((ROWS, E), f32),
            pltpu.VMEM((ROWS, E), f32),
            pltpu.VMEM((ROWS, E), f32),
            pltpu.VMEM((ROWS, E), f32),
            pltpu.VMEM((E + 8, E), f32),
            pltpu.VMEM((E + 8, E), f32),
            pltpu.VMEM((E, E), f32),
            pltpu.VMEM((E // 2, E), f32),
            dma((2,)),
            dma((CHIPS, 2)),
            dma((CHIPS, 2)),
            dma((CHIPS, 2)),
            dma((CHIPS, 2)),
            dma((2, 2)),
            dma((2, 2)),
            dma,
            dma,
            dma((2,)),
            dma((2,)),
        ],
        compiler_params=pltpu.CompilerParams(collective_id=0, has_side_effects=True),
        name="hybrid_heads",
    )(
        flat(lin_query), flat(lin_key), flat(lin_value), log_decay,
        flat(soft_query), flat(soft_key), flat(soft_value),
    )
    return lin.reshape(ROWS, 1, E), soft.reshape(ROWS, 1, E)


def solution(mesh):
    wide = P("ctx", "tp", None)
    return jax.shard_map(
        on_device,
        mesh=mesh,
        in_specs=(wide, wide, wide, P("tp", "ctx"), wide, wide, wide),
        out_specs=(wide, wide),
        check_vma=False,
    )
```

time: 394 us -> 52.2 us (0.13)
  the two profiles are of different devices: /device:TPU:1 before, /device:TPU:379 now
where the time goes in v1:
time: 52.2 us; the launch traced here: 52 us
  Pallas kernels  49.1 us (94%)
  local copies, waits for them, and re-layouts  2.26 us (4%)
  between operations  0.65 us (1%)
    pallas_call x1, Pallas kernels, on_device(): pl.pallas_call(kernel, out_shape=[jax.ShapeDtypeStruct((ROWS, E), bf16)]...  49.1 us
    unnamed x4, local copies, waits for them, and re-layouts  2.26 us

profile of v1, /device:TPU:379, one launch (start us, length us, event | category | flops | bytes accessed | tf_op | source)
XLA Modules:
  0.0 52.0 jit_solution(7394560403392069805)
XLA Ops:
  0.6 49.1 %hybrid_heads.1 = (bf16[512,128]{1,0:T(8,128)(2,1)}, bf16[512,128]{1,0:T(8,128)(2,1)}) custom-call(bf16[512,128]{1,0:T(8,128)(2,1)} %bitcast.10, bf16[512,128]{1,0:T(8,128)(2,1)} %bitcast.11, bf16[512,128]{1,0:T(8,128)(2,1)} %bitcast.12, f32[1,512]{1,0:T(1,128)} %ld.1, bf16[512,128]{1,0:T(8,128)(2,1)} %bitcast.13, bf16[512,128]{1,0:T(8,128)(2,1)} %bitcast.14, ...), custom_call_target="tpu_custom_call" | custom-call | tf_op jit(solution)/shard_map/hybrid_heads/pallas_call | solution.py:360
  49.8 0.0 copy-start
  49.8 1.6 %copy.11 = bf16[512,1,128]{2,0,1:T(8,128)(2,1)} copy(bf16[512,1,128]{2,0,1:T(8,128)(2,1)} %bitcast.9) | data formatting | bytes 262144
  51.4 0.0 copy-done
  51.4 0.7 %copy.12 = bf16[512,1,128]{2,0,1:T(8,128)(2,1)} copy(bf16[512,1,128]{2,0,1:T(8,128)(2,1)S(1)} %bitcast.8) | data formatting | bytes 262144
Async XLA Ops:
  49.8 1.6 %copy-start = (bf16[512,128]{1,0:T(8,128)(2,1)S(1)}, bf16[512,128]{1,0:T(8,128)(2,1)}, u32[]{:S(2)}) copy-start(bf16[512,128]{1,0:T(8,128)(2,1)} %get-tuple-element.5) | copy-start | bytes 393220

commit v2 on v1

v2 whole, which is shorter than its diff:
```python
import functools
import math

import jax
import jax.numpy as jnp
from jax import lax
from jax.experimental import pallas as pl
from jax.experimental.pallas import tpu as pltpu
from jax.sharding import PartitionSpec as P

MESH = pl.DeviceIdType.MESH
ROWS = 512
E = 128
CHIPS = 8
TILE = 128
HELPER = 1
FIRST_HELPED = 5
HELPED = CHIPS - FIRST_HELPED
STAT = 16
SCALE = math.log2(math.e) / math.sqrt(E)
NEG = -1e30


def dot_nt(a, b):
    return lax.dot_general(a, b, (((1,), (1,)), ((), ())), preferred_element_type=jnp.float32)


def dot_tn(a, b):
    return lax.dot_general(a, b, (((0,), (0,)), ((), ())), preferred_element_type=jnp.float32)


def dot_nn(a, b):
    return jnp.dot(a, b, preferred_element_type=jnp.float32)


def kernel(
    lq_hbm, lk_hbm, lv_hbm, ld_hbm, sq_hbm, sk, sv,
    lin_out, soft_out,
    lq, lk, lv, ld, sq,
    kv, far_query, far_out, near_out, far_top, far_total, far_summed,
    top, total, summed, intra, cumcol, state, sib_state, carry, onward,
    own_sem, up_send, z_recv, sib_send, sib_recv, q_send, q_recv, o_send, o_recv, x_send, x_recv,
    c_send, c_recv,
):
    me = lax.axis_index("ctx")
    k = me // 2
    c = me % 2
    sib = me + 1 - 2 * c

    helped = k >= FIRST_HELPED

    def to(ctx):
        return {"ctx": ctx}

    barrier = pltpu.get_barrier_semaphore()

    def greet(device):
        pl.semaphore_signal(barrier, inc=1, device_id=device, device_id_type=MESH)

    greet(to(sib))

    @pl.when(k > 0)
    def _():
        greet(to(me - 2))

    @pl.when(k == HELPER)
    def _():
        for j in range(HELPED):
            greet(to(2 * (FIRST_HELPED + j) + c))

    local = [
        pltpu.make_async_copy(src, dst, own_sem.at[i])
        for i, (src, dst) in enumerate((
            (ld_hbm, ld), (lk_hbm, lk), (lv_hbm, lv), (lq_hbm, lq), (sq_hbm, sq),
            (sk, kv.at[me, 0]), (sv, kv.at[me, 1]),
        ))
    ]
    for copy in local:
        copy.start()

    expected = 1 + jnp.where(k < CHIPS - 1, 1, 0) + jnp.where(helped, 1, 0)
    pl.semaphore_wait(barrier, expected)

    def remote(src, dst, send, recv, device):
        return pltpu.make_async_remote_copy(
            src_ref=src, dst_ref=dst, send_sem=send, recv_sem=recv,
            device_id=device, device_id_type=MESH,
        )

    def up_copy(src, b, t):
        return remote(src, kv.at[2 * b + c, t], up_send.at[b, t], z_recv.at[b, t], to(me + 2))

    def sib_copy(src, b, t):
        return remote(src, kv.at[2 * b + c, t], sib_send.at[b, t], sib_recv.at[b, t], to(sib))

    def query_copy(j):
        return remote(sq_hbm, far_query.at[j], q_send, q_recv.at[j], to(2 * HELPER + c))

    def out_copy(j):
        return remote(
            far_out.at[j], near_out, o_send.at[j], o_recv, to(2 * (FIRST_HELPED + j) + c)
        )

    own = (sk, sv)

    own_to_sib = (c == 0) | (k == HELPER)

    def send_own(t):
        @pl.when(k < CHIPS - 1)
        def _():
            up_copy(own[t], k, t).start()

        @pl.when(own_to_sib)
        def _():
            sib_copy(own[t], k, t).start()

    send_own(0)

    @pl.when(helped)
    def _():
        query_copy(k - FIRST_HELPED).start()

    for copy in local[:3]:
        copy.wait()

    cum = jnp.broadcast_to(ld[...], (8, ROWS))
    lane = lax.broadcasted_iota(jnp.int32, (8, ROWS), 1)
    shift = 1
    while shift < ROWS:
        cum = cum + jnp.where(lane >= shift, pltpu.roll(cum, shift, 1), 0.0)
        shift *= 2
    row = cum[0:1]
    cumcol[...] = jnp.transpose(jnp.broadcast_to(row, (E, ROWS)))
    last = cumcol[ROWS - 1:ROWS, :]
    decayed = (lk[...].astype(jnp.float32) * jnp.exp(last - cumcol[...])).astype(jnp.bfloat16)
    state[0:E, :] = dot_tn(decayed, lv[...])
    state[E:E + 8, :] = jnp.broadcast_to(jnp.exp(last), (8, E))
    exchange = remote(state, sib_state, x_send, x_recv, to(sib))
    exchange.start()

    @pl.when(k > 0)
    def _():
        send_own(1)

    half = E // 2

    def up_carry():
        return remote(
            onward, carry.at[pl.ds(c * half, half)], c_send.at[0], c_recv.at[0], to(me + 2)
        )

    def side_carry():
        return remote(
            carry.at[pl.ds(c * half, half)], carry.at[pl.ds(c * half, half)],
            c_send.at[1], c_recv.at[1], to(sib),
        )

    def chip_state():
        even = jnp.where(c == 0, 1.0, 0.0)
        odd = 1.0 - even
        f_me = state[E:E + 1, :]
        f_sib = sib_state[E:E + 1, :]
        mine = state[pl.ds(c * half, half), :]
        theirs = sib_state[pl.ds(c * half, half), :]
        f_odd = f_me * odd + f_sib * even
        s_even = mine * even + theirs * odd
        s_odd = mine * odd + theirs * even
        return f_me * f_sib, f_odd * s_even + s_odd

    exchange.wait_recv()

    @pl.when(k == 0)
    def _():
        carry[...] = jnp.zeros((E, E), jnp.float32)
        onward[...] = chip_state()[1]
        up_carry().start()

    def pass_carry():
        up_carry().wait_recv()
        side_carry().start()

        @pl.when(k < CHIPS - 1)
        def _():
            factor, added = chip_state()
            onward[...] = factor * carry[pl.ds(c * half, half), :] + added
            up_carry().start()

    @pl.when(k == 0)
    def _():
        send_own(1)

    for copy in local[3:]:
        copy.wait()

    lower = (
        lax.broadcasted_iota(jnp.int32, (TILE, TILE), 0)
        >= lax.broadcasted_iota(jnp.int32, (TILE, TILE), 1)
    )
    for r in range(ROWS // TILE):
        mine = slice(r * TILE, (r + 1) * TILE)
        part = jnp.zeros((TILE, E), jnp.float32)
        for s in range(r + 1):
            theirs = slice(s * TILE, (s + 1) * TILE)
            diff = cumcol[mine, :] - row[:, theirs]
            if s == r:
                diff = jnp.where(lower, diff, NEG)
            weight = (dot_nt(lq[mine, :], lk[theirs, :]) * jnp.exp(diff)).astype(jnp.bfloat16)
            part = part + dot_nn(weight, lv[theirs, :])
        intra[mine, :] = part

    for r in range(ROWS // TILE):
        mine = slice(r * TILE, (r + 1) * TILE)
        reach = (r + 1) * TILE
        score = dot_nt(sq[mine, :], kv[me, 0, 0:reach, :]) * SCALE
        allowed = (
            lax.broadcasted_iota(jnp.int32, (TILE, reach), 0) + r * TILE
            >= lax.broadcasted_iota(jnp.int32, (TILE, reach), 1)
        )
        score = jnp.where(allowed, score, NEG)
        peak = jnp.broadcast_to(jnp.max(score, axis=1, keepdims=True), (TILE, E))
        prob = jnp.exp2(score - jnp.concatenate([peak] * (r + 1), axis=1))
        top[mine, :] = peak
        total[mine, :] = jnp.broadcast_to(jnp.sum(prob, axis=1, keepdims=True), (TILE, E))
        summed[mine, :] = dot_nn(prob.astype(jnp.bfloat16), kv[me, 1, 0:reach, :])

    def update(slot, query, top, total, summed):
        keys = kv[slot, 0]
        values = kv[slot, 1]
        for r in range(ROWS // TILE):
            mine = slice(r * TILE, (r + 1) * TILE)
            score = dot_nt(query[mine, :], keys) * SCALE
            before = top[mine, :]
            peak = jnp.maximum(before, jnp.max(score, axis=1, keepdims=True))
            prob = jnp.exp2(score - jnp.concatenate([peak] * (ROWS // E), axis=1))
            fade = jnp.exp2(before - peak)
            top[mine, :] = peak
            total[mine, :] = total[mine, :] * fade + jnp.sum(prob, axis=1, keepdims=True)
            summed[mine, :] = summed[mine, :] * fade + dot_nn(prob.astype(jnp.bfloat16), values)

    @pl.when(c == 1)
    def _():
        for t in range(2):
            sib_copy(kv.at[me - 1, t], k, t).wait_recv()
        update(me - 1, sq, top, total, summed)

    def sends_up(b):
        return (k < FIRST_HELPED - 1) | ((k < CHIPS - 1) & (b > HELPER))

    def step(s, _):
        b = k - s
        for t in range(2):
            up_copy(kv.at[2 * b + c, t], b, t).wait_recv()

            @pl.when(sends_up(b))
            def _(t=t):
                up_copy(kv.at[2 * b + c, t], b, t).start()

            sib_copy(kv.at[2 * b + c, t], b, t).start()
            if t == 0:
                @pl.when(b == 0)
                def _():
                    pass_carry()

        update(2 * b + c, sq, top, total, summed)
        for t in range(2):
            sib_copy(kv.at[2 * b + 1 - c, t], b, t).wait_recv()
        update(2 * b + 1 - c, sq, top, total, summed)
        return 0

    lax.fori_loop(1, jnp.where(helped, k - HELPER, k + 1), step, 0)

    @pl.when(helped)
    def _():
        pass_carry()

    tiles = [slice(r * TILE, (r + 1) * TILE) for r in range(ROWS // TILE)]

    @pl.when(k == HELPER)
    def _():
        for t in range(2):
            @pl.when(c == 0)
            def _(t=t):
                sib_copy(kv.at[me + 1, t], k, t).wait_recv()

        def one(i, _):
            j = HELPED - 1 - i
            query_copy(j).wait_recv()
            far_top[...] = jnp.full((ROWS, E), NEG, jnp.float32)
            far_total[...] = jnp.zeros((ROWS, E), jnp.float32)
            far_summed[...] = jnp.zeros((ROWS, E), jnp.float32)

            def over(u, _):
                update(2 * HELPER + 1 - u, far_query.at[j], far_top, far_total, far_summed)
                return 0

            lax.fori_loop(0, 2 * HELPER + 2, over, 0)
            stats = []
            for mine in tiles:
                far_out[j, mine, :] = (far_summed[mine, :] / far_total[mine, :]).astype(jnp.bfloat16)
                level = far_top[mine, :] + jnp.log2(far_total[mine, :])
                stats.append(jnp.transpose(level)[0:1, :])
            level = jnp.concatenate(stats, axis=0)
            high = level.astype(jnp.bfloat16).astype(jnp.float32)
            middle = (level - high).astype(jnp.bfloat16).astype(jnp.float32)
            low = level - high - middle
            far_out[j, ROWS:ROWS + STAT, :] = jnp.concatenate(
                [high, middle, low, jnp.zeros_like(low)], axis=0
            ).astype(jnp.bfloat16)
            out_copy(j).start()
            return 0

        lax.fori_loop(0, HELPED, one, 0)

    @pl.when(helped)
    def _():
        out_copy(0).wait_recv()
        parts = near_out[ROWS:ROWS + STAT, :].astype(jnp.float32)
        level = parts[0:4] + parts[4:8] + parts[8:12]
        for r, mine in enumerate(tiles):
            arrived = jnp.transpose(jnp.broadcast_to(level[r:r + 1, :], (TILE, E)))
            before = top[mine, :]
            peak = jnp.maximum(before, arrived)
            fade = jnp.exp2(before - peak)
            share = jnp.exp2(arrived - peak)
            total[mine, :] = total[mine, :] * fade + share
            summed[mine, :] = summed[mine, :] * fade + near_out[mine, :].astype(jnp.float32) * share

    for r in range(ROWS // TILE):
        mine = slice(r * TILE, (r + 1) * TILE)
        soft_out[mine, :] = (summed[mine, :] / total[mine, :]).astype(soft_out.dtype)

    @pl.when(k > 0)
    def _():
        side_carry().wait_recv()

    even = jnp.where(c == 0, 1.0, 0.0)
    odd = 1.0 - even
    f_sib = sib_state[E:E + 1, :]
    entering = (
        carry[...] * (even + odd * f_sib) + odd * sib_state[0:E, :]
    ).astype(jnp.bfloat16)
    for r in range(ROWS // TILE):
        mine = slice(r * TILE, (r + 1) * TILE)
        raw = intra[mine, :] + dot_nn(lq[mine, :], entering) * jnp.exp(cumcol[mine, :])
        mean = jnp.mean(raw * raw, axis=1, keepdims=True)
        lin_out[mine, :] = (raw * lax.rsqrt(mean + 1e-06)).astype(lin_out.dtype)

    exchange.wait_send()

    @pl.when(k < CHIPS - 1)
    def _():
        up_carry().wait_send()

    @pl.when(k > 0)
    def _():
        side_carry().wait_send()

    def drain(b, _):
        for t in range(2):
            @pl.when(sends_up(b))
            def _(t=t):
                up_copy(kv.at[2 * b + c, t], b, t).wait_send()

            @pl.when((b < k) | own_to_sib)
            def _(t=t):
                sib_copy(kv.at[2 * b + c, t], b, t).wait_send()
        return 0

    lax.fori_loop(jnp.where(helped, HELPER + 1, 0), k + 1, drain, 0)

    @pl.when(helped)
    def _():
        query_copy(0).wait_send()

    @pl.when(k == HELPER)
    def _():
        for j in range(HELPED):
            out_copy(j).wait_send()


def on_device(lin_query, lin_key, lin_value, log_decay, soft_query, soft_key, soft_value):
    def stay(array):
        return pltpu.with_memory_space_constraint(array, pltpu.MemorySpace.HBM)

    def flat(array):
        return stay(array.reshape(ROWS, E))

    vmem = pl.BlockSpec(memory_space=pltpu.VMEM)
    hbm = pl.BlockSpec(memory_space=pltpu.MemorySpace.HBM)
    f32, bf16 = jnp.float32, jnp.bfloat16
    dma = pltpu.SemaphoreType.DMA
    lin, soft = pl.pallas_call(
        kernel,
        out_shape=[jax.ShapeDtypeStruct((ROWS, E), bf16)] * 2,
        in_specs=[hbm] * 7,
        out_specs=[vmem] * 2,
        scratch_shapes=[
            pltpu.VMEM((ROWS, E), bf16),
            pltpu.VMEM((ROWS, E), bf16),
            pltpu.VMEM((ROWS, E), bf16),
            pltpu.VMEM((1, ROWS), f32),
            pltpu.VMEM((ROWS, E), bf16),
            pltpu.VMEM((2 * CHIPS, 2, ROWS, E), bf16),
            pltpu.VMEM((HELPED, ROWS, E), bf16),
            pltpu.VMEM((HELPED, ROWS + STAT, E), bf16),
            pltpu.VMEM((ROWS + STAT, E), bf16),
            pltpu.VMEM((ROWS, E), f32),
            pltpu.VMEM((ROWS, E), f32),
            pltpu.VMEM((ROWS, E), f32),
            pltpu.VMEM((ROWS, E), f32),
            pltpu.VMEM((ROWS, E), f32),
            pltpu.VMEM((ROWS, E), f32),
            pltpu.VMEM((ROWS, E), f32),
            pltpu.VMEM((ROWS, E), f32),
            pltpu.VMEM((E + 8, E), f32),
            pltpu.VMEM((E + 8, E), f32),
            pltpu.VMEM((E, E), f32),
            pltpu.VMEM((E // 2, E), f32),
            dma((7,)),
            dma((CHIPS, 2)),
            dma((CHIPS, 2)),
            dma((CHIPS, 2)),
            dma((CHIPS, 2)),
            dma,
            dma((HELPED,)),
            dma((HELPED,)),
            dma,
            dma,
            dma,
            dma((2,)),
            dma((2,)),
        ],
        compiler_params=pltpu.CompilerParams(
            collective_id=0, has_side_effects=True, vmem_limit_bytes=24 << 20
        ),
        name="hybrid_heads",
    )(
        flat(lin_query), flat(lin_key), flat(lin_value), stay(log_decay),
        flat(soft_query), flat(soft_key), flat(soft_value),
    )
    return lin.reshape(ROWS, 1, E), soft.reshape(ROWS, 1, E)


def solution(mesh):
    wide = P("ctx", "tp", None)
    return jax.shard_map(
        on_device,
        mesh=mesh,
        in_specs=(wide, wide, wide, P("tp", "ctx"), wide, wide, wide),
        out_specs=(wide, wide),
        check_vma=False,
    )
```

time: 52.2 us -> 46.1 us (0.88)
  the two profiles are of different devices: /device:TPU:379 before, /device:TPU:961 now
where the time goes in v2:
time: 46.1 us; the launch traced here: 45.9 us
  Pallas kernels  44 us (95%)
  local copies, waits for them, and re-layouts  1.31 us (3%)
  between operations  0.64 us (1%)
    pallas_call x1, Pallas kernels, on_device(): pl.pallas_call(kernel, out_shape=[jax.ShapeDtypeStruct((ROWS, E), bf16)]...  44 us
    unnamed x2, local copies, waits for them, and re-layouts  1.31 us

profile of v2, /device:TPU:961, one launch (start us, length us, event | category | flops | bytes accessed | tf_op | source)
XLA Modules:
  0.0 45.9 jit_solution(14178620735232880950)
XLA Ops:
  0.6 44.0 %hybrid_heads.1 = (bf16[512,128]{1,0:T(8,128)(2,1)S(1)}, bf16[512,128]{1,0:T(8,128)(2,1)S(1)}) custom-call(bf16[512,128]{1,0:T(8,128)(2,1)} %bitcast.10, bf16[512,128]{1,0:T(8,128)(2,1)} %bitcast.11, bf16[512,128]{1,0:T(8,128)(2,1)} %bitcast.12, f32[1,512]{1,0:T(1,128)} %ld_hbm.1, bf16[512,128]{1,0:T(8,128)(2,1)} %bitcast.13, bf16[512,128]{1,0:T(8,128)(2,1)} %bitcast.14, ...), custom_call_target="tpu_custom_call" | custom-call | tf_op jit(solution)/shard_map/hybrid_heads/pallas_call | solution.py:392
  44.6 0.7 %copy.11 = bf16[512,1,128]{2,0,1:T(8,128)(2,1)} copy(bf16[512,1,128]{2,0,1:T(8,128)(2,1)S(1)} %bitcast.9) | data formatting | bytes 262144
  45.3 0.7 %copy.12 = bf16[512,1,128]{2,0,1:T(8,128)(2,1)} copy(bf16[512,1,128]{2,0,1:T(8,128)(2,1)S(1)} %bitcast.8) | data formatting | bytes 262144

commit v3 on v2

--- a/solution.py
+++ b/solution.py
@@ -38,7 +38,7 @@
     lin_out, soft_out,
     lq, lk, lv, ld, sq,
     kv, far_query, far_out, near_out, far_top, far_total, far_summed,
-    top, total, summed, intra, cumcol, state, sib_state, carry, onward,
+    weights, fades, top, total, summed, intra, cumcol, state, sib_state, carry, onward,
     own_sem, up_send, z_recv, sib_send, sib_recv, q_send, q_recv, o_send, o_recv, x_send, x_recv,
     c_send, c_recv,
 ):
@@ -223,9 +223,12 @@
         total[mine, :] = jnp.broadcast_to(jnp.sum(prob, axis=1, keepdims=True), (TILE, E))
         summed[mine, :] = dot_nn(prob.astype(jnp.bfloat16), kv[me, 1, 0:reach, :])
 
+    def with_ones(values):
+        return jnp.concatenate([values, jnp.ones_like(values)], axis=1)
+
     def update(slot, query, top, total, summed):
         keys = kv[slot, 0]
-        values = kv[slot, 1]
+        values = with_ones(kv[slot, 1])
         for r in range(ROWS // TILE):
             mine = slice(r * TILE, (r + 1) * TILE)
             score = dot_nt(query[mine, :], keys) * SCALE
@@ -234,8 +237,30 @@
             prob = jnp.exp2(score - jnp.concatenate([peak] * (ROWS // E), axis=1))
             fade = jnp.exp2(before - peak)
             top[mine, :] = peak
-            total[mine, :] = total[mine, :] * fade + jnp.sum(prob, axis=1, keepdims=True)
-            summed[mine, :] = summed[mine, :] * fade + dot_nn(prob.astype(jnp.bfloat16), values)
+            added = dot_nn(prob.astype(jnp.bfloat16), values)
+            total[mine, :] = total[mine, :] * fade + added[:, E:]
+            summed[mine, :] = summed[mine, :] * fade + added[:, 0:E]
+
+    def weigh(slot, u):
+        keys = kv[slot, 0]
+        for r in range(ROWS // TILE):
+            mine = slice(r * TILE, (r + 1) * TILE)
+            score = dot_nt(sq[mine, :], keys) * SCALE
+            before = top[mine, :]
+            peak = jnp.maximum(before, jnp.max(score, axis=1, keepdims=True))
+            prob = jnp.exp2(score - jnp.concatenate([peak] * (ROWS // E), axis=1))
+            fade = jnp.exp2(before - peak)
+            top[mine, :] = peak
+            weights[u, mine, :] = prob.astype(jnp.bfloat16)
+            fades[u, mine, :] = fade
+
+    def gather(slot, u):
+        values = with_ones(kv[slot, 1])
+        for r in range(ROWS // TILE):
+            mine = slice(r * TILE, (r + 1) * TILE)
+            added = dot_nn(weights[u, mine, :], values)
+            summed[mine, :] = summed[mine, :] * fades[u, mine, :] + added[:, 0:E]
+            total[mine, :] = total[mine, :] * fades[u, mine, :] + added[:, E:]
 
     @pl.when(c == 1)
     def _():
@@ -246,25 +271,34 @@
     def sends_up(b):
         return (k < FIRST_HELPED - 1) | ((k < CHIPS - 1) & (b > HELPER))
 
+    def arrive(b, t):
+        up_copy(kv.at[2 * b + c, t], b, t).wait_recv()
+
+        @pl.when(sends_up(b))
+        def _():
+            up_copy(kv.at[2 * b + c, t], b, t).start()
+
+        sib_copy(kv.at[2 * b + c, t], b, t).start()
+
+    @pl.when(k == 1)
+    def _():
+        pass_carry()
+
     def step(s, _):
         b = k - s
-        for t in range(2):
-            up_copy(kv.at[2 * b + c, t], b, t).wait_recv()
-
-            @pl.when(sends_up(b))
-            def _(t=t):
-                up_copy(kv.at[2 * b + c, t], b, t).start()
-
-            sib_copy(kv.at[2 * b + c, t], b, t).start()
-            if t == 0:
-                @pl.when(b == 0)
-                def _():
-                    pass_carry()
-
-        update(2 * b + c, sq, top, total, summed)
-        for t in range(2):
-            sib_copy(kv.at[2 * b + 1 - c, t], b, t).wait_recv()
-        update(2 * b + 1 - c, sq, top, total, summed)
+        arrive(b, 0)
+        weigh(2 * b + c, 0)
+        sib_copy(kv.at[2 * b + 1 - c, 0], b, 0).wait_recv()
+        weigh(2 * b + 1 - c, 1)
+        arrive(b, 1)
+
+        @pl.when((k > 1) & (b == 1))
+        def _():
+            pass_carry()
+
+        gather(2 * b + c, 0)
+        sib_copy(kv.at[2 * b + 1 - c, 1], b, 1).wait_recv()
+        gather(2 * b + 1 - c, 1)
         return 0
 
     lax.fori_loop(1, jnp.where(helped, k - HELPER, k + 1), step, 0)
@@ -407,6 +441,8 @@
             pltpu.VMEM((ROWS, E), f32),
             pltpu.VMEM((ROWS, E), f32),
             pltpu.VMEM((ROWS, E), f32),
+            pltpu.VMEM((2, ROWS, ROWS), bf16),
+            pltpu.VMEM((2, ROWS, E), f32),
             pltpu.VMEM((ROWS, E), f32),
             pltpu.VMEM((ROWS, E), f32),
             pltpu.VMEM((ROWS, E), f32),

time: 46.1 us -> 45.1 us (0.978)
  the two profiles are of different devices: /device:TPU:961 before, /device:TPU:257 now
where the time goes in v3:
time: 45.1 us; the launch traced here: 44.9 us
  Pallas kernels  43 us (95%)
  local copies, waits for them, and re-layouts  1.31 us (3%)
  between operations  0.64 us (1%)
    pallas_call x1, Pallas kernels, on_device(): pl.pallas_call(kernel, out_shape=[jax.ShapeDtypeStruct((ROWS, E), bf16)]...  43 us
    unnamed x2, local copies, waits for them, and re-layouts  1.31 us

profile of v3, /device:TPU:257, one launch (start us, length us, event | category | flops | bytes accessed | tf_op | source)
XLA Modules:
  0.0 44.9 jit_solution(10525254510199095182)
XLA Ops:
  0.6 43.0 %hybrid_heads.1 = (bf16[512,128]{1,0:T(8,128)(2,1)S(1)}, bf16[512,128]{1,0:T(8,128)(2,1)S(1)}) custom-call(bf16[512,128]{1,0:T(8,128)(2,1)} %bitcast.10, bf16[512,128]{1,0:T(8,128)(2,1)} %bitcast.11, bf16[512,128]{1,0:T(8,128)(2,1)} %bitcast.12, f32[1,512]{1,0:T(1,128)} %ld_hbm.1, bf16[512,128]{1,0:T(8,128)(2,1)} %bitcast.13, bf16[512,128]{1,0:T(8,128)(2,1)} %bitcast.14, ...), custom_call_target="tpu_custom_call" | custom-call | tf_op jit(solution)/shard_map/hybrid_heads/pallas_call | solution.py:426
  43.6 0.7 %copy.11 = bf16[512,1,128]{2,0,1:T(8,128)(2,1)} copy(bf16[512,1,128]{2,0,1:T(8,128)(2,1)S(1)} %bitcast.9) | data formatting | bytes 262144
  44.3 0.7 %copy.12 = bf16[512,1,128]{2,0,1:T(8,128)(2,1)} copy(bf16[512,1,128]{2,0,1:T(8,128)(2,1)S(1)} %bitcast.8) | data formatting | bytes 262144

commit v4 on v3

--- a/solution.py
+++ b/solution.py
@@ -40,9 +40,10 @@
     kv, far_query, far_out, near_out, far_top, far_total, far_summed,
     weights, fades, top, total, summed, intra, cumcol, state, sib_state, carry, onward,
     own_sem, up_send, z_recv, sib_send, sib_recv, q_send, q_recv, o_send, o_recv, x_send, x_recv,
-    c_send, c_recv,
+    c_send, c_recv, ready,
 ):
     me = lax.axis_index("ctx")
+    late = lax.axis_index("tp") == 0
     k = me // 2
     c = me % 2
     sib = me + 1 - 2 * c
@@ -57,7 +58,9 @@
     def greet(device):
         pl.semaphore_signal(barrier, inc=1, device_id=device, device_id_type=MESH)
 
-    greet(to(sib))
+    @pl.when(jnp.logical_not(late & (me == 0)))
+    def _():
+        greet(to(sib))
 
     @pl.when(k > 0)
     def _():
@@ -78,8 +81,13 @@
     for copy in local:
         copy.start()
 
-    expected = 1 + jnp.where(k < CHIPS - 1, 1, 0) + jnp.where(helped, 1, 0)
+    expected = jnp.where(late & (me == 1), 0, 1) + jnp.where(k < CHIPS - 1, 1, 0) + jnp.where(helped, 1, 0)
     pl.semaphore_wait(barrier, expected)
+
+    @pl.when(late & (me == 0))
+    def _():
+        pl.semaphore_signal(ready, inc=1, device_id=to(sib), device_id_type=MESH)
+
 
     def remote(src, dst, send, recv, device):
         return pltpu.make_async_remote_copy(
@@ -136,6 +144,12 @@
     state[0:E, :] = dot_tn(decayed, lv[...])
     state[E:E + 8, :] = jnp.broadcast_to(jnp.exp(last), (8, E))
     exchange = remote(state, sib_state, x_send, x_recv, to(sib))
+
+    @pl.when(late & (me == 1))
+    def _():
+        send_own(1)
+        pl.semaphore_wait(ready, 1)
+
     exchange.start()
 
     @pl.when(k > 0)
@@ -185,7 +199,7 @@
             onward[...] = factor * carry[pl.ds(c * half, half), :] + added
             up_carry().start()
 
-    @pl.when(k == 0)
+    @pl.when((k == 0) & jnp.logical_not(late & (me == 1)))
     def _():
         send_own(1)
 
@@ -280,7 +294,7 @@
 
         sib_copy(kv.at[2 * b + c, t], b, t).start()
 
-    @pl.when(k == 1)
+    @pl.when((k == 1) & jnp.logical_not(late))
     def _():
         pass_carry()
 
@@ -288,11 +302,20 @@
         b = k - s
         arrive(b, 0)
         weigh(2 * b + c, 0)
+        early = late & (b == 0)
+
+        @pl.when(early)
+        def _():
+            arrive(b, 1)
+
         sib_copy(kv.at[2 * b + 1 - c, 0], b, 0).wait_recv()
         weigh(2 * b + 1 - c, 1)
-        arrive(b, 1)
-
-        @pl.when((k > 1) & (b == 1))
+
+        @pl.when(jnp.logical_not(early))
+        def _():
+            arrive(b, 1)
+
+        @pl.when(early | ((k > 1) & (b == 1) & jnp.logical_not(late)))
         def _():
             pass_carry()
 
@@ -465,6 +488,7 @@
             dma,
             dma((2,)),
             dma((2,)),
+            pltpu.SemaphoreType.REGULAR,
         ],
         compiler_params=pltpu.CompilerParams(
             collective_id=0, has_side_effects=True, vmem_limit_bytes=24 << 20

time: 45.1 us -> 45.9 us (1.018)
  the two profiles are of different devices: /device:TPU:257 before, /device:TPU:449 now
where the time goes in v4:
time: 45.9 us; the launch traced here: 45.8 us
  Pallas kernels  43.8 us (95%)
  local copies, waits for them, and re-layouts  1.31 us (3%)
  between operations  0.64 us (1%)
    pallas_call x1, Pallas kernels, on_device(): pl.pallas_call(kernel, out_shape=[jax.ShapeDtypeStruct((ROWS, E), bf16)]...  43.8 us
    unnamed x2, local copies, waits for them, and re-layouts  1.31 us

profile of v4, /device:TPU:449, one launch (start us, length us, event | category | flops | bytes accessed | tf_op | source)
XLA Modules:
  0.0 45.8 jit_solution(17740594024038075855)
XLA Ops:
  0.6 43.8 %hybrid_heads.1 = (bf16[512,128]{1,0:T(8,128)(2,1)S(1)}, bf16[512,128]{1,0:T(8,128)(2,1)S(1)}) custom-call(bf16[512,128]{1,0:T(8,128)(2,1)} %bitcast.10, bf16[512,128]{1,0:T(8,128)(2,1)} %bitcast.11, bf16[512,128]{1,0:T(8,128)(2,1)} %bitcast.12, f32[1,512]{1,0:T(1,128)} %ld_hbm.1, bf16[512,128]{1,0:T(8,128)(2,1)} %bitcast.13, bf16[512,128]{1,0:T(8,128)(2,1)} %bitcast.14, ...), custom_call_target="tpu_custom_call" | custom-call | tf_op jit(solution)/shard_map/hybrid_heads/pallas_call | solution.py:449
  44.4 0.7 %copy.11 = bf16[512,1,128]{2,0,1:T(8,128)(2,1)} copy(bf16[512,1,128]{2,0,1:T(8,128)(2,1)S(1)} %bitcast.9) | data formatting | bytes 262144
  45.1 0.7 %copy.12 = bf16[512,1,128]{2,0,1:T(8,128)(2,1)} copy(bf16[512,1,128]{2,0,1:T(8,128)(2,1)S(1)} %bitcast.8) | data formatting | bytes 262144

commit v5 on v4

--- a/solution.py
+++ b/solution.py
@@ -300,14 +300,22 @@
 
     def step(s, _):
         b = k - s
+        early = late & (b == 0)
         arrive(b, 0)
+
+        @pl.when(early & (c == 1))
+        def _():
+            arrive(b, 1)
+
+        @pl.when(early)
+        def _():
+            pass_carry()
+
+        @pl.when(early & (c == 0))
+        def _():
+            arrive(b, 1)
+
         weigh(2 * b + c, 0)
-        early = late & (b == 0)
-
-        @pl.when(early)
-        def _():
-            arrive(b, 1)
-
         sib_copy(kv.at[2 * b + 1 - c, 0], b, 0).wait_recv()
         weigh(2 * b + 1 - c, 1)
 
@@ -315,7 +323,7 @@
         def _():
             arrive(b, 1)
 
-        @pl.when(early | ((k > 1) & (b == 1) & jnp.logical_not(late)))
+        @pl.when((k > 1) & (b == 1) & jnp.logical_not(late))
         def _():
             pass_carry()
 

time: 45.9 us -> 44 us (0.959)
  Pallas kernels: 43.8 us -> 41.9 us
    pallas_call x1, Pallas kernels: 43.8 us -> 41.9 us  [on_device(): pl.pallas_call(kernel, out_shape=[jax.ShapeDtypeStruct((ROWS, E), bf16)]...]
where the time goes in v5:
time: 44 us; the launch traced here: 43.9 us
  Pallas kernels  41.9 us (95%)
  local copies, waits for them, and re-layouts  1.31 us (3%)
  between operations  0.64 us (1%)
    pallas_call x1, Pallas kernels, on_device(): pl.pallas_call(kernel, out_shape=[jax.ShapeDtypeStruct((ROWS, E), bf16)]...  41.9 us
    unnamed x2, local copies, waits for them, and re-layouts  1.31 us

profile of v5, /device:TPU:449, one launch (start us, length us, event | category | flops | bytes accessed | tf_op | source)
XLA Modules:
  0.0 43.9 jit_solution(13938761606714515167)
XLA Ops:
  0.6 41.9 %hybrid_heads.1 = (bf16[512,128]{1,0:T(8,128)(2,1)S(1)}, bf16[512,128]{1,0:T(8,128)(2,1)S(1)}) custom-call(bf16[512,128]{1,0:T(8,128)(2,1)} %bitcast.10, bf16[512,128]{1,0:T(8,128)(2,1)} %bitcast.11, bf16[512,128]{1,0:T(8,128)(2,1)} %bitcast.12, f32[1,512]{1,0:T(1,128)} %ld_hbm.1, bf16[512,128]{1,0:T(8,128)(2,1)} %bitcast.13, bf16[512,128]{1,0:T(8,128)(2,1)} %bitcast.14, ...), custom_call_target="tpu_custom_call" | custom-call | tf_op jit(solution)/shard_map/hybrid_heads/pallas_call | solution.py:457
  42.5 0.7 %copy.11 = bf16[512,1,128]{2,0,1:T(8,128)(2,1)} copy(bf16[512,1,128]{2,0,1:T(8,128)(2,1)S(1)} %bitcast.9) | data formatting | bytes 262144
  43.2 0.7 %copy.12 = bf16[512,1,128]{2,0,1:T(8,128)(2,1)} copy(bf16[512,1,128]{2,0,1:T(8,128)(2,1)S(1)} %bitcast.8) | data formatting | bytes 262144
